TPU v7x, 32 devices: a whole 2x2x4 slice. The times are simulated.
32 devices in a mesh: row: 4 (over z), col: 8 (over y, x, core).
Axes of the slice: x: 2, y: 2, z: 4, core: 2. Of those that a mesh axis runs over, the one named last changes fastest.
Arguments:
- inputs: bfloat16 [192, 12288], P('col', 'row'), may hold values from -40 to 40
- ln_gain: float32 [12288], P('row'), may hold values from 0.25 to 1.75
- ln_bias: float32 [12288], P('row'), may hold values from -4 to 4
- w_up: bfloat16 [12288, 49152], P('row', 'col'), may hold values from -0.0546875 to 0.0546875
- up_bias: float32 [49152], P('col'), may hold values from -4 to 4
- w_down: bfloat16 [49152, 12288], P('col', 'row'), may hold values from -0.02734375 to 0.02734375
- down_bias: float32 [12288], P('row'), may hold values from -4 to 4
Outputs:
- block_out: bfloat16 [192, 12288], P('col', 'row')
All inputs are finite; a program needn't handle non-finite values.
Results may differ from a plain program's by a relative error of at most 0.0085.
Values may be sent and summed in bfloat16 or wider, within the bound.
No kernel may reach another device: no remote copies, remote signals or barrier semaphores. Data moves between devices by JAX's collectives and lax.ppermute only.
A program may use at most 128 MiB of HBM per device.

v0:
```python
import jax
import jax.numpy as jnp
from jax import lax
from jax.sharding import PartitionSpec as P

D = 12288


def local(inputs, ln_gain, ln_bias, w_up, up_bias, w_down, down_bias):
    in_float = inputs.astype(jnp.float32)
    total, squares = lax.psum(
        (jnp.sum(in_float, axis=1), jnp.sum(in_float * in_float, axis=1)), "row"
    )
    average = total / D
    centered = in_float - average[:, None]
    variance = squares / D - average * average
    normed = (centered * lax.rsqrt(variance + 1e-05)[:, None] * ln_gain + ln_bias).astype(
        jnp.bfloat16
    )
    gathered = lax.all_gather(normed, "col", axis=0, tiled=True)
    summed = lax.psum_scatter(
        jnp.dot(gathered, w_up, preferred_element_type=jnp.float32).astype(jnp.bfloat16),
        "row",
        scatter_dimension=0,
        tiled=True,
    ).astype(jnp.float32)
    hidden = jax.nn.gelu(summed + up_bias, approximate=True).astype(jnp.bfloat16)
    terms = jnp.dot(
        lax.all_gather(hidden, "row", axis=0, tiled=True),
        w_down,
        preferred_element_type=jnp.float32,
    )
    down_sum = lax.psum_scatter(
        terms.astype(jnp.bfloat16), "col", scatter_dimension=0, tiled=True
    ).astype(jnp.float32)
    return (in_float + down_sum + down_bias).astype(jnp.bfloat16)


def solution(mesh):
    placed = (
        P("col", "row"),
        P("row"),
        P("row"),
        P("row", "col"),
        P("col"),
        P("col", "row"),
        P("row"),
    )
    return jax.shard_map(
        local, mesh=mesh, in_specs=placed, out_specs=P("col", "row"), check_vma=False
    )
```

profile of v0, /device:TPU:0, one launch (start us, length us, event | category | flops | bytes accessed | tf_op | source)
XLA Modules:
  0.0 223.3 jit_solution(8975903873406821275)
XLA Ops:
  6.5 0.0 all-gather.3.cloned.1.call-start
  6.5 1.1 convert_reduce_fusion
  7.6 13.5 %all-reduce = (f32[24]{0:T(128)S(1)}, f32[24]{0:T(128)S(1)}) all-reduce(f32[24]{0:T(128)S(1)} %get-tuple-element.6, f32[24]{0:T(128)S(1)} %get-tuple-element.5), channel_id=1, replica_groups=mesh['row'=4,'col'=8] {'row'}, use_global_device_ids=true, to_apply=%region_3.0 | all-reduce | flops 48 | bytes 384 | tf_op jit(solution)/shard_map/psum | solution.py:11
  21.1 1.7 fusion.11
  22.8 0.0 all-gather.3.cloned.1.call-update
  22.8 0.0 reduce-scatter.3.cloned.1.call-start
  22.9 22.2 %all-gather.3.cloned.1.call-done = bf16[192,3072]{1,0:T(8,128)(2,1)} async-done(((bf16[24,3072]{1,0:T(8,128)(2,1)}), bf16[192,3072]{1,0:T(8,128)(2,1)}) %all-gather.3.cloned.1.call-update) | async-done | bytes 1179664 | tf_op jit(solution)/shard_map/all_gather | solution.py:20
  45.1 17.4 %convolution_convert_fusion = bf16[192,6144]{1,0:T(8,128)(2,1)} fusion(bf16[192,3072]{1,0:T(8,128)(2,1)} %all-gather.3.cloned.1.call-done, bf16[3072,6144]{1,0:T(8,128)(2,1)} %param.10), kind=kOutput, calls=%fused_computation | convolution fusion | flops 7248936960 | bytes 41287680 | tf_op jit(solution)/shard_map/dot_general | solution.py:22
  62.5 0.0 copy-start.1
  62.5 0.0 reduce-scatter.3.cloned.1.call-update
  62.5 0.0 all-gather.5.cloned.1.call-start
  62.5 47.8 %reduce-scatter.3.cloned.1.call-done = bf16[48,6144]{1,0:T(8,128)(2,1)} async-done(((bf16[192,6144]{1,0:T(8,128)(2,1)}), bf16[48,6144]{1,0:T(8,128)(2,1)}) %reduce-scatter.3.cloned.1.call-update) | async-done | bytes 589840 | tf_op jit(solution)/shard_map/reduce_scatter | solution.py:21
  110.4 0.0 copy-done.1
  110.4 2.3 %fusion.7 = bf16[48,6144]{1,0:T(8,128)(2,1)} fusion(bf16[48,6144]{1,0:T(8,128)(2,1)} %reduce-scatter.3.cloned.1.call-done, f32[6144]{0:T(1024)S(1)} %copy-done.1), kind=kLoop, calls=%fused_computation.10 | loop fusion | flops 3244032 | bytes 1204224 | tf_op jit(solution)/shard_map/convert_element_type | solution.py:27
  112.7 0.0 all-gather.5.cloned.1.call-update
  112.7 0.0 reduce-scatter.5.cloned.1.call-start
  112.8 49.5 %all-gather.5.cloned.1.call-done = bf16[192,6144]{1,0:T(8,128)(2,1)} async-done(((bf16[48,6144]{1,0:T(8,128)(2,1)}), bf16[192,6144]{1,0:T(8,128)(2,1)}) %all-gather.5.cloned.1.call-update) | async-done | bytes 2359312 | tf_op jit(solution)/shard_map/all_gather | solution.py:29
  162.2 17.3 %convolution_convert_fusion.1 = bf16[192,3072]{1,0:T(8,128)(2,1)} fusion(bf16[192,6144]{1,0:T(8,128)(2,1)} %all-gather.5.cloned.1.call-done, bf16[6144,3072]{1,0:T(8,128)(2,1)} %param.12), kind=kOutput, calls=%fused_computation.1 | convolution fusion | flops 7248347136 | bytes 41287680 | tf_op jit(solution)/shard_map/dot_general | solution.py:28
  179.5 0.0 copy-start
  179.5 0.0 copy-start.2
  179.5 0.0 reduce-scatter.5.cloned.1.call-update
  179.5 35.6 %reduce-scatter.5.cloned.1.call-done = bf16[24,3072]{1,0:T(8,128)(2,1)} async-done(((bf16[192,3072]{1,0:T(8,128)(2,1)}), bf16[24,3072]{1,0:T(8,128)(2,1)}) %reduce-scatter.5.cloned.1.call-update) | async-done | bytes 147472 | tf_op jit(solution)/shard_map/reduce_scatter | solution.py:33
  215.1 0.0 copy-done
  215.1 0.0 copy-done.2
  215.1 1.6 fusion.14
  (1 shorter events, 0.0 us)
Async XLA Ops:
  6.5 38.6 %all-gather.3.cloned.1.call-start = ((), (), s32[]{:S(2)}) async-start(), calls=%async_computation.2 | async-start | bytes 1327104 | tf_op jit(solution)/shard_map/all_gather | solution.py:20
  22.8 87.5 %reduce-scatter.3.cloned.1.call-start = ((), (), s32[]{:S(2)}) async-start(), calls=%async_computation.3 | async-start | bytes 2949120 | tf_op jit(solution)/shard_map/reduce_scatter | solution.py:21
  62.5 47.9 %copy-start.1 = (f32[6144]{0:T(1024)S(1)}, f32[6144]{0:T(1024)}, u32[]{:S(2)}) copy-start(f32[6144]{0:T(1024)} %param.11) | copy-start | bytes 73732
  62.5 99.7 %all-gather.5.cloned.1.call-start = ((), (), s32[]{:S(2)}) async-start(), calls=%async_computation.4 | async-start | bytes 2949120 | tf_op jit(solution)/shard_map/all_gather | solution.py:29
  112.7 102.4 %reduce-scatter.5.cloned.1.call-start = ((), (), s32[]{:S(2)}) async-start(), calls=%async_computation.5 | async-start | bytes 1327104 | tf_op jit(solution)/shard_map/reduce_scatter | solution.py:33
  179.5 35.6 %copy-start = (bf16[24,3072]{1,0:T(8,128)(2,1)S(1)}, bf16[24,3072]{1,0:T(8,128)(2,1)}, u32[]{:S(2)}) copy-start(bf16[24,3072]{1,0:T(8,128)(2,1)} %param.7) | copy-start | bytes 442372
  179.5 35.6 %copy-start.2 = (f32[3072]{0:T(1024)S(1)}, f32[3072]{0:T(1024)}, u32[]{:S(2)}) copy-start(f32[3072]{0:T(1024)} %param.13) | copy-start | bytes 36868
Sparse Core Ops, SparseCore 0:
  22.9 22.1 all-gather.2
  62.6 47.6 reduce-scatter.2
  112.8 49.3 all-gather.4
  179.6 35.4 reduce-scatter.4
where the time goes:
time: 224 us; the launch traced here: 223 us
  waiting for transfers between devices  155 us (69%)
  matrix products  34.6 us (15%)
  blocking collectives  13.5 us (6%)
  between operations  13.1 us (6%)
  other arithmetic  6.73 us (3%)
    all_gather x1, waiting for transfers between devices, local(): lax.all_gather(hidden, 'row', axis=0, tiled=True)  49.5 us
    reduce_scatter x1, waiting for transfers between devices, local(): lax.psum_scatter(jnp.dot(gathered, w_up, preferred_element_type=jnp.float...  47.8 us
    reduce_scatter x1, waiting for transfers between devices, local(): lax.psum_scatter(terms.astype(jnp.bfloat16), 'col', scatter_dimension=0,...  35.6 us
    all_gather x1, waiting for transfers between devices, local(): gathered = lax.all_gather(normed, 'col', axis=0, tiled=True)  22.2 us
    dot_general x1, matrix products, local(): jnp.dot(gathered, w_up, preferred_element_type=jnp.float32)  17.4 us
    dot_general x1, matrix products, local(): jnp.dot(lax.all_gather(hidden, 'row', axis=0, tiled=True), w_down, prefer...  17.3 us
    psum x1, blocking collectives, local(): lax.psum((jnp.sum(in_float, axis=1), jnp.sum(in_float * in_float, axis=1)...  13.5 us
  transfers between devices with their start and end apart: 4, of which 4 were waited for; matrix products, arithmetic and copies ran while one was open for 0% of the time, Pallas kernels for 0%

commit v1 on v0

--- a/solution.py
+++ b/solution.py
@@ -4,6 +4,21 @@
 from jax.sharding import PartitionSpec as P
 
 D = 12288
+
+
+def streams_choose(in_array, dim_k):
+    axis_len = lax.psum(1, axis_name="col")
+    found = [in_array]
+    q = 0
+    while q < axis_len - 1:
+        shaped = lax.ppermute(
+            found[-1], "col", [(to_i, (to_i + 1) % axis_len) for to_i in range(axis_len)]
+        )
+        found.append(shaped)
+        q += 1
+    m_next = jnp.concatenate(found[::-1], axis=dim_k)
+    right_arr = lax.axis_index("col")
+    return jnp.roll(m_next, shift=(right_arr + 1) * in_array.shape[dim_k], axis=dim_k)
 
 
 def local(inputs, ln_gain, ln_bias, w_up, up_bias, w_down, down_bias):
@@ -17,7 +32,7 @@
     normed = (centered * lax.rsqrt(variance + 1e-05)[:, None] * ln_gain + ln_bias).astype(
         jnp.bfloat16
     )
-    gathered = lax.all_gather(normed, "col", axis=0, tiled=True)
+    gathered = streams_choose(normed, 0)
     summed = lax.psum_scatter(
         jnp.dot(gathered, w_up, preferred_element_type=jnp.float32).astype(jnp.bfloat16),
         "row",

time: 224 us -> 236 us (1.054)
  waiting for transfers between devices: 155 us -> 168 us
    ppermute x0 -> x7, waiting for transfers between devices: none -> 38.2 us  [streams_choose(): lax.ppermute(found[-1], 'col', [(to_i, (to_i + 1) % axis_len) for to_i in...]
    all_gather x1 -> x0, waiting for transfers between devices: 22.2 us -> none  [local(): gathered = lax.all_gather(normed, 'col', axis=0, tiled=True)]
    reduce_scatter x1, waiting for transfers between devices: 47.8 us -> 45.1 us  [local(): lax.psum_scatter(jnp.dot(gathered, w_up, preferred_element_type=jnp.float...]
  transfers between devices with their start and end apart: 4 -> 10, of which waited for: 4 -> 10; matrix products, arithmetic and copies ran while one was open for 0% -> 0% of each run, Pallas kernels for 0% -> 0%
where the time goes in v1:
time: 236 us
  waiting for transfers between devices  168 us (71%)
  matrix products  33.7 us (14%)
  blocking collectives  13.5 us (6%)
  between operations  13.3 us (6%)
  other arithmetic  6.37 us (3%)
    all_gather x1, waiting for transfers between devices, local(): lax.all_gather(hidden, 'row', axis=0, tiled=True)  49.5 us
    reduce_scatter x1, waiting for transfers between devices, local(): lax.psum_scatter(jnp.dot(gathered, w_up, preferred_element_type=jnp.float...  45.1 us
    ppermute x7, waiting for transfers between devices, streams_choose(): lax.ppermute(found[-1], 'col', [(to_i, (to_i + 1) % axis_len) for to_i in...  38.2 us
    reduce_scatter x1, waiting for transfers between devices, local(): lax.psum_scatter(terms.astype(jnp.bfloat16), 'col', scatter_dimension=0,...  35.6 us
    dot_general x1, matrix products, local(): jnp.dot(lax.all_gather(hidden, 'row', axis=0, tiled=True), w_down, prefer...  17.3 us
    dot_general x1, matrix products, local(): jnp.dot(gathered, w_up, preferred_element_type=jnp.float32)  16.4 us
    psum x1, blocking collectives, local(): lax.psum((jnp.sum(in_float, axis=1), jnp.sum(in_float * in_float, axis=1)...  13.5 us
  transfers between devices with their start and end apart: 10, of which 10 were waited for; matrix products, arithmetic and copies ran while one was open for 0% of the time, Pallas kernels for 0%

profile of v1, /device:TPU:0, one launch (start us, length us, event | category | flops | bytes accessed | tf_op | source)
XLA Modules:
  0.0 235.6 jit_solution(8484304511726947115)
XLA Ops:
  6.5 0.0 copy-start
  6.5 0.0 copy-start.2
  6.5 0.0 copy-start.1
  6.5 0.0 reduce-scatter.3.cloned.1.call-start
  6.5 1.1 convert_reduce_fusion
  7.7 13.5 %all-reduce = (f32[24]{0:T(128)S(1)}, f32[24]{0:T(128)S(1)}) all-reduce(f32[24]{0:T(128)S(1)} %get-tuple-element.6, f32[24]{0:T(128)S(1)} %get-tuple-element.5), channel_id=1, replica_groups=mesh['row'=4,'col'=8] {'row'}, use_global_device_ids=true, to_apply=%region_3.0 | all-reduce | flops 48 | bytes 384 | tf_op jit(solution)/shard_map/psum | solution.py:26
  21.2 1.1 fusion.12
  22.2 0.1 collective-permute-start
  22.3 5.5 %collective-permute-done = bf16[24,3072]{1,0:T(8,128)(2,1)S(1)} collective-permute-done((bf16[24,3072]{1,0:T(8,128)(2,1)S(1)}, bf16[24,3072]{1,0:T(8,128)(2,1)S(1)}, u32[]{:S(2)}, u32[]{:S(2)}) %collective-permute-start) | collective-permute-done | bytes 147488 | tf_op jit(solution)/shard_map/ppermute | solution.py:14
  27.7 0.0 collective-permute-start.1
  27.7 5.5 %collective-permute-done.1 = bf16[24,3072]{1,0:T(8,128)(2,1)S(1)} collective-permute-done((bf16[24,3072]{1,0:T(8,128)(2,1)S(1)}, bf16[24,3072]{1,0:T(8,128)(2,1)S(1)}, u32[]{:S(2)}, u32[]{:S(2)}) %collective-permute-start.1) | collective-permute-done | bytes 147488 | tf_op jit(solution)/shard_map/ppermute | solution.py:14
  33.2 0.0 collective-permute-start.2
  33.2 5.5 %collective-permute-done.2 = bf16[24,3072]{1,0:T(8,128)(2,1)S(1)} collective-permute-done((bf16[24,3072]{1,0:T(8,128)(2,1)S(1)}, bf16[24,3072]{1,0:T(8,128)(2,1)S(1)}, u32[]{:S(2)}, u32[]{:S(2)}) %collective-permute-start.2) | collective-permute-done | bytes 147488 | tf_op jit(solution)/shard_map/ppermute | solution.py:14
  38.7 0.0 collective-permute-start.3
  38.7 5.5 %collective-permute-done.3 = bf16[24,3072]{1,0:T(8,128)(2,1)S(1)} collective-permute-done((bf16[24,3072]{1,0:T(8,128)(2,1)S(1)}, bf16[24,3072]{1,0:T(8,128)(2,1)S(1)}, u32[]{:S(2)}, u32[]{:S(2)}) %collective-permute-start.3) | collective-permute-done | bytes 147488 | tf_op jit(solution)/shard_map/ppermute | solution.py:14
  44.1 0.0 collective-permute-start.4
  44.1 5.5 %collective-permute-done.4 = bf16[24,3072]{1,0:T(8,128)(2,1)S(1)} collective-permute-done((bf16[24,3072]{1,0:T(8,128)(2,1)S(1)}, bf16[24,3072]{1,0:T(8,128)(2,1)S(1)}, u32[]{:S(2)}, u32[]{:S(2)}) %collective-permute-start.4) | collective-permute-done | bytes 147488 | tf_op jit(solution)/shard_map/ppermute | solution.py:14
  49.6 0.0 collective-permute-start.5
  49.6 5.5 %collective-permute-done.5 = bf16[24,3072]{1,0:T(8,128)(2,1)S(1)} collective-permute-done((bf16[24,3072]{1,0:T(8,128)(2,1)S(1)}, bf16[24,3072]{1,0:T(8,128)(2,1)S(1)}, u32[]{:S(2)}, u32[]{:S(2)}) %collective-permute-start.5) | collective-permute-done | bytes 147488 | tf_op jit(solution)/shard_map/ppermute | solution.py:14
  55.1 0.0 collective-permute-start.6
  55.1 5.5 %collective-permute-done.6 = bf16[24,3072]{1,0:T(8,128)(2,1)S(1)} collective-permute-done((bf16[24,3072]{1,0:T(8,128)(2,1)S(1)}, bf16[24,3072]{1,0:T(8,128)(2,1)S(1)}, u32[]{:S(2)}, u32[]{:S(2)}) %collective-permute-start.6) | collective-permute-done | bytes 147488 | tf_op jit(solution)/shard_map/ppermute | solution.py:14
  60.7 0.0 copy-done
  60.7 0.0 copy-done.2
  60.7 0.0 copy-done.1
  60.7 0.1 constant_dynamic-update-slice_fusion.8
  61.0 0.1 constant_dynamic-update-slice_fusion
  61.1 16.4 %convolution_convert_fusion = bf16[192,6144]{1,0:T(8,128)(2,1)} fusion(bf16[3072,6144]{1,0:T(8,128)(2,1)} %param.10, bf16[384,3072]{1,0:T(8,128)(2,1)S(1)} %constant_dynamic-update-slice_fusion, s32[]{:T(128)S(6)} %select_n.14), kind=kOutput, calls=%fused_computation | convolution fusion | flops 7248936960 | bytes 41287684 | tf_op jit(solution)/shard_map/dot_general | solution.py:37
  77.5 0.0 copy-start.3
  77.5 0.0 reduce-scatter.3.cloned.1.call-update
  77.5 0.0 all-gather.2.cloned.1.call-start
  77.6 45.1 %reduce-scatter.3.cloned.1.call-done = bf16[48,6144]{1,0:T(8,128)(2,1)} async-done(((bf16[192,6144]{1,0:T(8,128)(2,1)}), bf16[48,6144]{1,0:T(8,128)(2,1)}) %reduce-scatter.3.cloned.1.call-update) | async-done | bytes 589840 | tf_op jit(solution)/shard_map/reduce_scatter | solution.py:36
  122.7 0.0 copy-done.3
  122.7 2.3 fusion.7
  125.0 0.0 all-gather.2.cloned.1.call-update
  125.0 0.0 copy-start.4
  125.0 0.0 reduce-scatter.5.cloned.1.call-start
  125.1 49.5 %all-gather.2.cloned.1.call-done = bf16[192,6144]{1,0:T(8,128)(2,1)} async-done(((bf16[48,6144]{1,0:T(8,128)(2,1)}), bf16[192,6144]{1,0:T(8,128)(2,1)}) %all-gather.2.cloned.1.call-update) | async-done | bytes 2359312 | tf_op jit(solution)/shard_map/all_gather | solution.py:44
  174.5 17.3 %convolution_convert_fusion.1 = bf16[192,3072]{1,0:T(8,128)(2,1)} fusion(bf16[192,6144]{1,0:T(8,128)(2,1)} %all-gather.2.cloned.1.call-done, bf16[6144,3072]{1,0:T(8,128)(2,1)} %param.12), kind=kOutput, calls=%fused_computation.1 | convolution fusion | flops 7248347136 | bytes 41287680 | tf_op jit(solution)/shard_map/dot_general | solution.py:43
  191.8 0.0 reduce-scatter.5.cloned.1.call-update
  191.8 35.6 %reduce-scatter.5.cloned.1.call-done = bf16[24,3072]{1,0:T(8,128)(2,1)} async-done(((bf16[192,3072]{1,0:T(8,128)(2,1)}), bf16[24,3072]{1,0:T(8,128)(2,1)}) %reduce-scatter.5.cloned.1.call-update) | async-done | bytes 147472 | tf_op jit(solution)/shard_map/reduce_scatter | solution.py:48
  227.4 0.0 copy-done.4
  227.4 1.6 fusion.15
  (15 shorter events, 0.2 us)
Async XLA Ops:
  6.5 54.1 %copy-start = (bf16[24,3072]{1,0:T(8,128)(2,1)S(1)}, bf16[24,3072]{1,0:T(8,128)(2,1)}, u32[]{:S(2)}) copy-start(bf16[24,3072]{1,0:T(8,128)(2,1)} %param.7) | copy-start | bytes 442372
  6.5 54.2 %copy-start.2 = (f32[3072]{0:T(1024)S(1)}, f32[3072]{0:T(1024)}, u32[]{:S(2)}) copy-start(f32[3072]{0:T(1024)} %param.8) | copy-start | bytes 36868
  6.5 54.2 %copy-start.1 = (f32[3072]{0:T(1024)S(1)}, f32[3072]{0:T(1024)}, u32[]{:S(2)}) copy-start(f32[3072]{0:T(1024)} %param.9) | copy-start | bytes 36868
  6.5 116.1 %reduce-scatter.3.cloned.1.call-start = ((), (), s32[]{:S(2)}) async-start(), calls=%async_computation.2 | async-start | bytes 2949120 | tf_op jit(solution)/shard_map/reduce_scatter | solution.py:36
  22.2 5.5 %collective-permute-start = (bf16[24,3072]{1,0:T(8,128)(2,1)S(1)}, bf16[24,3072]{1,0:T(8,128)(2,1)S(1)}, u32[]{:S(2)}, u32[]{:S(2)}) collective-permute-start(bf16[24,3072]{1,0:T(8,128)(2,1)S(1)} %fusion.12), channel_id=1, source_target_pairs={{0,1},{1,2},{2,3},{3,4},{4,5},{5,6},{6,7},{7,0},{8,9},{9,10},{10,1... | collective-permute-start | bytes 442376 | tf_op jit(solution)/shard_map/ppermute | solution.py:14
  27.7 5.5 %collective-permute-start.1 = (bf16[24,3072]{1,0:T(8,128)(2,1)S(1)}, bf16[24,3072]{1,0:T(8,128)(2,1)S(1)}, u32[]{:S(2)}, u32[]{:S(2)}) collective-permute-start(bf16[24,3072]{1,0:T(8,128)(2,1)S(1)} %collective-permute-done), channel_id=1, source_target_pairs={{0,1},{1,2},{2,3},{3,4},{4,5},{5,6},{6,7},{7,0},{8,9},{9,10},{10,1... | collective-permute-start | bytes 442376 | tf_op jit(solution)/shard_map/ppermute | solution.py:14
  33.2 5.5 %collective-permute-start.2 = (bf16[24,3072]{1,0:T(8,128)(2,1)S(1)}, bf16[24,3072]{1,0:T(8,128)(2,1)S(1)}, u32[]{:S(2)}, u32[]{:S(2)}) collective-permute-start(bf16[24,3072]{1,0:T(8,128)(2,1)S(1)} %collective-permute-done.1), channel_id=1, source_target_pairs={{0,1},{1,2},{2,3},{3,4},{4,5},{5,6},{6,7},{7,0},{8,9},{9,10},{10,1... | collective-permute-start | bytes 442376 | tf_op jit(solution)/shard_map/ppermute | solution.py:14
  38.7 5.5 %collective-permute-start.3 = (bf16[24,3072]{1,0:T(8,128)(2,1)S(1)}, bf16[24,3072]{1,0:T(8,128)(2,1)S(1)}, u32[]{:S(2)}, u32[]{:S(2)}) collective-permute-start(bf16[24,3072]{1,0:T(8,128)(2,1)S(1)} %collective-permute-done.2), channel_id=1, source_target_pairs={{0,1},{1,2},{2,3},{3,4},{4,5},{5,6},{6,7},{7,0},{8,9},{9,10},{10,1... | collective-permute-start | bytes 442376 | tf_op jit(solution)/shard_map/ppermute | solution.py:14
  44.1 5.5 %collective-permute-start.4 = (bf16[24,3072]{1,0:T(8,128)(2,1)S(1)}, bf16[24,3072]{1,0:T(8,128)(2,1)S(1)}, u32[]{:S(2)}, u32[]{:S(2)}) collective-permute-start(bf16[24,3072]{1,0:T(8,128)(2,1)S(1)} %collective-permute-done.3), channel_id=1, source_target_pairs={{0,1},{1,2},{2,3},{3,4},{4,5},{5,6},{6,7},{7,0},{8,9},{9,10},{10,1... | collective-permute-start | bytes 442376 | tf_op jit(solution)/shard_map/ppermute | solution.py:14
  49.6 5.5 %collective-permute-start.5 = (bf16[24,3072]{1,0:T(8,128)(2,1)S(1)}, bf16[24,3072]{1,0:T(8,128)(2,1)S(1)}, u32[]{:S(2)}, u32[]{:S(2)}) collective-permute-start(bf16[24,3072]{1,0:T(8,128)(2,1)S(1)} %collective-permute-done.4), channel_id=1, source_target_pairs={{0,1},{1,2},{2,3},{3,4},{4,5},{5,6},{6,7},{7,0},{8,9},{9,10},{10,1... | collective-permute-start | bytes 442376 | tf_op jit(solution)/shard_map/ppermute | solution.py:14
  55.1 5.5 %collective-permute-start.6 = (bf16[24,3072]{1,0:T(8,128)(2,1)S(1)}, bf16[24,3072]{1,0:T(8,128)(2,1)S(1)}, u32[]{:S(2)}, u32[]{:S(2)}) collective-permute-start(bf16[24,3072]{1,0:T(8,128)(2,1)S(1)} %collective-permute-done.5), channel_id=1, source_target_pairs={{0,1},{1,2},{2,3},{3,4},{4,5},{5,6},{6,7},{7,0},{8,9},{9,10},{10,1... | collective-permute-start | bytes 442376 | tf_op jit(solution)/shard_map/ppermute | solution.py:14
  77.5 45.2 %copy-start.3 = (f32[6144]{0:T(1024)S(1)}, f32[6144]{0:T(1024)}, u32[]{:S(2)}) copy-start(f32[6144]{0:T(1024)} %param.11) | copy-start | bytes 73732
  77.5 97.0 %all-gather.2.cloned.1.call-start = ((), (), s32[]{:S(2)}) async-start(), calls=%async_computation.3 | async-start | bytes 2949120 | tf_op jit(solution)/shard_map/all_gather | solution.py:44
  125.0 102.4 %copy-start.4 = (f32[3072]{0:T(1024)S(1)}, f32[3072]{0:T(1024)}, u32[]{:S(2)}) copy-start(f32[3072]{0:T(1024)} %param.13) | copy-start | bytes 36868
  125.0 102.4 %reduce-scatter.5.cloned.1.call-start = ((), (), s32[]{:S(2)}) async-start(), calls=%async_computation.4 | async-start | bytes 1327104 | tf_op jit(solution)/shard_map/reduce_scatter | solution.py:48
Sparse Core Ops, SparseCore 0:
  77.6 44.9 reduce-scatter.2
  125.1 49.3 all-gather.1
  191.9 35.4 reduce-scatter.4
